TPU v7x, 256 devices: a whole 4x4x8 slice. The times are simulated.
256 devices in a mesh: head: 4 (over x), page: 64 (over y, z, core).
Axes of the slice: x: 4, y: 4, z: 8, core: 2. Of those that a mesh axis runs over, the one named last changes fastest.
Arguments:
- hidden: bfloat16 [12, 2048], P(None, 'page'), may hold values from -6 to 6
- q_weight: bfloat16 [2048, 3072], P('page', 'head'), may hold values from -0.125 to 0.125
- key_up: bfloat16 [16, 128, 512], P('head'), may hold values from -0.5 to 0.5
- value_up_weight: bfloat16 [16, 512, 128], P('head'), may hold values from -0.25 to 0.25
- out_weight: bfloat16 [2048, 2048], P('head', 'page'), may hold values from -0.125 to 0.125
- cache: bfloat16 [16, 512, 128, 576], P('head', 'page'), may hold values from -360 to 360
- page_table: int32 [16, 512], P('head', 'page'), may hold values from 0 to 511, each once within a row
- seq_pages: int32 [12], replicated, may hold values from 1 to 128, 512 in all
- keep_rows: int32 [16, 512, 64], P('head'), may hold values from 0 to 127, as said below
- fold_mass: bfloat16 [16, 512, 64], P('head'), may hold values from 0.5 to 4
- new_place: int32 [16, 512], P('head'), may hold values from 0 to 2047, as said below
- norm_gain: bfloat16 [2048], replicated, may hold values from 0.099609375 to 1.8984375
- router: bfloat16 [2048, 64], replicated, may hold values from -0.125 to 0.125
- routes: int32 [12, 6], replicated, may hold values from 0 to 63, all different within a row
- w_gate: bfloat16 [64, 2048, 1408], P('page', None, 'head'), may hold values from -0.125 to 0.125
- w_up: bfloat16 [64, 2048, 1408], P('page', None, 'head'), may hold values from -0.125 to 0.125
- w_down: bfloat16 [64, 1408, 2048], P('page', 'head'), may hold values from -0.15625 to 0.15625
Outputs:
- attn_out: bfloat16 [12, 2048], replicated
- moe_out: bfloat16 [12, 2048], replicated
- new_rows: bfloat16 [8192, 64, 576], P(('head', 'page'))
- new_mass: bfloat16 [8192, 64], P(('head', 'page'))
Inputs may be any that keep to these rules, and one draw needn't show every extreme that they name: `keep_rows`: the 64 entries of each head and page are distinct. `new_place`: for each group of heads h // 4 the places form a permutation of 0 to 2047. Among the blocks of one head group whose pages share g // 8, at most 1 have places with the same place // 32, and some reach 1.
All inputs are finite; a program needn't handle non-finite values.
Results may differ from a plain program's by a relative error of at most 0.035.
Values may be sent and summed in bfloat16 or wider, within the bound.
A program may use at most 128 MiB of HBM per device.

v0:
```python
import jax
import jax.numpy as jnp
from jax import lax
from jax.sharding import PartitionSpec as P

QK_NOPE = 128
QK_ROPE = 64
THETA = 50000.0
ROUTE_SCALE = 2.446
NORM_EPS = 1e-06


def joined_2(part, axis, combine):
    gathered = jax.tree.map(lambda a: lax.all_gather(a, axis), part)

    def take(source):
        return jax.tree.map(lambda a: lax.dynamic_index_in_dim(a, source, 0, False), gathered)

    return lax.fori_loop(
        1, lax.axis_size(axis), lambda source, state: combine(state, take(source)), take(0)
    )


def rotate_query(values, positions):
    half_dim = values.shape[-1] // 2
    freqs = THETA ** (-2.0 * jnp.arange(half_dim, dtype=jnp.float32) / values.shape[-1])
    angles = positions.astype(jnp.float32)[:, None] * freqs[None, :]
    cosine = jnp.cos(angles)[:, None, :]
    sine_v = jnp.sin(angles)[:, None, :]
    front = values[..., :half_dim]
    back = values[..., half_dim:]
    return jnp.concatenate(
        [front * cosine - back * sine_v, back * cosine + front * sine_v], axis=-1
    )


def pick_rows(one_page, row_ids):
    return one_page[row_ids]


def merge_parts(left_part, right_part):
    joined = jnp.maximum(left_part[0], right_part[0])
    left_factor = jnp.exp(left_part[0] - joined)
    right_factor = jnp.exp(right_part[0] - joined)
    return (
        joined,
        left_part[1] * left_factor + right_part[1] * right_factor,
        left_part[2] * left_factor[..., None] + right_part[2] * right_factor[..., None],
    )


def shards(
    hidden,
    q_weight,
    key_up,
    value_up_weight,
    out_weight,
    cache,
    page_table,
    seq_pages,
    keep_rows,
    fold_mass,
    new_place,
    norm_gain,
    router,
    routes,
    w_gate,
    w_up,
    w_down,
):
    heads_here = key_up.shape[0]
    pages_here = cache.shape[1]
    page_rows = cache.shape[2]
    latent_dim = cache.shape[3]
    kv_rank = key_up.shape[2]
    kept_count = keep_rows.shape[2]
    requests = hidden.shape[0]
    head_size = QK_NOPE + QK_ROPE
    groups = lax.axis_size("page")
    page_index = lax.axis_index("page")
    blocks = heads_here * pages_here
    sending_limit = (blocks + groups - 1) // groups
    first_page = page_index * pages_here
    partial_value = jnp.dot(hidden, q_weight, preferred_element_type=jnp.float32)
    queries = lax.psum(partial_value, "page").reshape(requests, heads_here, head_size)
    q_nope = queries[..., :QK_NOPE].astype(jnp.bfloat16)
    positions = seq_pages * page_rows - 1
    q_rope = rotate_query(queries[..., QK_NOPE:], positions).astype(jnp.bfloat16)
    q_latent = jnp.einsum(
        "rhn,hnk->rhk", q_nope, key_up, preferred_element_type=jnp.float32
    ).astype(jnp.bfloat16)
    q_full = jnp.concatenate([q_latent, q_rope], axis=-1)
    keep_here = lax.dynamic_slice_in_dim(keep_rows, first_page, pages_here, 1)
    mass_here = lax.dynamic_slice_in_dim(fold_mass, first_page, pages_here, 1)
    compact = jax.vmap(jax.vmap(pick_rows))(cache, keep_here)
    flat_rows = compact.reshape(heads_here, pages_here * kept_count, latent_dim)
    page_ends = jnp.cumsum(seq_pages)
    owner = jnp.sum((page_table[..., None] >= page_ends).astype(jnp.int32), axis=-1)
    row_owner = jnp.repeat(owner, kept_count, axis=1)
    in_request = row_owner[:, None, :] == jnp.arange(requests, dtype=jnp.int32)[None, :, None]
    scores = jnp.einsum(
        "rhk,hnk->hrn", q_full, flat_rows, preferred_element_type=jnp.float32
    ) * head_size ** (-0.5)
    row_max = jnp.max(jnp.where(in_request, scores, -1e30), axis=-1)
    row_mass = mass_here.reshape(heads_here, 1, pages_here * kept_count).astype(jnp.float32)
    weights = jnp.where(in_request, row_mass * jnp.exp(scores - row_max[..., None]), 0.0)
    totals = jnp.sum(weights, axis=-1)
    weighted = jnp.einsum(
        "hrn,hnk->hrk",
        weights.astype(jnp.bfloat16),
        flat_rows[..., :kv_rank],
        preferred_element_type=jnp.float32,
    )
    best, mass_sum, latent_sum = joined_2((row_max, totals, weighted), "page", merge_parts)
    latent_output = (latent_sum / mass_sum[..., None]).astype(jnp.bfloat16)
    head_result_rows = jnp.einsum(
        "usj,ujb->sub", latent_output, value_up_weight, preferred_element_type=jnp.float32
    ).astype(jnp.bfloat16)
    head_result_rows = head_result_rows.reshape(requests, heads_here * value_up_weight.shape[2])
    out_cols = jnp.dot(head_result_rows, out_weight, preferred_element_type=jnp.float32)
    col_width = out_cols.shape[1]
    padded = jnp.zeros((requests, col_width * groups), jnp.float32)
    padded = lax.dynamic_update_slice_in_dim(padded, out_cols, page_index * col_width, 1)
    attn_out = lax.psum(padded, ("head", "page")).astype(jnp.bfloat16)
    attn_wide = attn_out.astype(jnp.float32)
    mean_sq = jnp.mean(attn_wide * attn_wide, axis=-1, keepdims=True)
    normed = (attn_wide * lax.rsqrt(mean_sq + NORM_EPS) * norm_gain.astype(jnp.float32)).astype(
        jnp.bfloat16
    )
    logits = jnp.dot(normed, router, preferred_element_type=jnp.float32)
    picked = jax.nn.sigmoid(jnp.take_along_axis(logits, routes, axis=1))
    shares = ROUTE_SCALE * picked / jnp.sum(picked, axis=1, keepdims=True)
    expert_ids = jnp.arange(logits.shape[1], dtype=jnp.int32)
    combine = jnp.sum(
        jnp.where(routes[:, :, None] == expert_ids[None, None, :], shares[:, :, None], 0.0), axis=1
    )
    local_experts = w_gate.shape[0]
    combine_here = lax.dynamic_slice_in_dim(combine, page_index * local_experts, local_experts, 1)
    gate_part = jnp.einsum("rd,edf->erf", normed, w_gate, preferred_element_type=jnp.float32)
    up_part = jnp.einsum("rd,edf->erf", normed, w_up, preferred_element_type=jnp.float32)
    expert_hidden = (jax.nn.silu(gate_part) * up_part).astype(jnp.bfloat16)
    expert_outs = jnp.einsum(
        "erf,efd->erd", expert_hidden, w_down, preferred_element_type=jnp.float32
    )
    expert_terms = jnp.sum(combine_here.T[:, :, None] * expert_outs, axis=0)
    moe_out = lax.psum(expert_terms, ("head", "page")).astype(jnp.bfloat16)
    dest_all = new_place // blocks
    slot_all = new_place % blocks
    dest_here = lax.dynamic_slice_in_dim(dest_all, first_page, pages_here, 1).reshape(blocks)
    peer_ids = jnp.arange(groups, dtype=jnp.int32)
    dest_onehot = (dest_here[:, None] == peer_ids[None, :]).astype(jnp.int32)
    send_rank = jnp.sum(jnp.cumsum(dest_onehot, axis=0) * dest_onehot, axis=1) - 1
    send_col = dest_here * sending_limit + send_rank
    slot_ids = jnp.arange(groups * sending_limit, dtype=jnp.int32)
    chooser = (send_col[:, None] == slot_ids[None, :]).astype(jnp.bfloat16)

    def arrange(values):
        return (
            values.reshape(heads_here, groups, pages_here)
            .transpose(1, 0, 2)
            .reshape(groups, blocks)
        )

    to_here = arrange(dest_all) == page_index
    recv_rank = jnp.cumsum(to_here.astype(jnp.int32), axis=1) - 1
    recv_col = peer_ids[:, None] * sending_limit + recv_rank
    block_ids = jnp.arange(blocks, dtype=jnp.int32)
    by_slot = ((arrange(slot_all)[..., None] == block_ids) & to_here[..., None]).astype(
        jnp.bfloat16
    )
    by_col = (recv_col[..., None] == slot_ids).astype(jnp.bfloat16)
    unpack = jnp.einsum("sbq,sbc->qc", by_slot, by_col, preferred_element_type=jnp.float32).astype(
        jnp.bfloat16
    )
    owned = (slot_all.reshape(-1)[None, :] == block_ids[:, None]) & (
        dest_all.reshape(-1)[None, :] == page_index
    )
    new_mass = jnp.dot(
        owned.astype(jnp.bfloat16),
        fold_mass.reshape(-1, kept_count),
        preferred_element_type=jnp.float32,
    ).astype(jnp.bfloat16)
    payload = cache.reshape(blocks, page_rows * latent_dim)
    outgoing = jnp.einsum("bc,bx->cx", chooser, payload, preferred_element_type=jnp.float32).astype(
        jnp.bfloat16
    )
    arrived_rows = lax.all_to_all(
        outgoing.reshape(groups, sending_limit, page_rows, latent_dim),
        "page",
        split_axis=0,
        concat_axis=0,
        tiled=True,
    )
    placed = jnp.dot(
        unpack,
        arrived_rows.reshape(groups * sending_limit, page_rows * latent_dim),
        preferred_element_type=jnp.float32,
    ).astype(jnp.bfloat16)
    keep_new = jnp.dot(owned.astype(jnp.int32), keep_rows.reshape(-1, kept_count))
    new_rows = jax.vmap(pick_rows)(placed.reshape(blocks, page_rows, latent_dim), keep_new)
    return (attn_out, moe_out, new_rows, new_mass)


def solution(mesh):
    in_specs = (
        P(None, "page"),
        P("page", "head"),
        P("head", None, None),
        P("head", None, None),
        P("head", "page"),
        P("head", "page", None, None),
        P("head", "page"),
        P(),
        P("head", None, None),
        P("head", None, None),
        P("head", None),
        P(),
        P(),
        P(),
        P("page", None, "head"),
        P("page", None, "head"),
        P("page", "head", None),
    )
    out_specs = (P(), P(), P(("head", "page"), None, None), P(("head", "page"), None))
    return jax.shard_map(shards, mesh=mesh, in_specs=in_specs, out_specs=out_specs, check_vma=False)
```

profile of v0, /device:TPU:1, one launch (start us, length us, event | category | flops | bytes accessed | tf_op | source)
XLA Modules:
  0.0 994.9 jit_solution(4305672104055780673)
XLA Ops:
  7.3 1.1 constant_dynamic-slice_fusion.2
  8.6 7.8 copy.109
  16.6 249.7 %psum.21 = f32[12,4,192]{2,0,1:T(8,128)S(1)} all-reduce(f32[12,4,192]{2,0,1:T(8,128)S(1)} %copy.107), channel_id=1, replica_groups=mesh['head'=4,'page'=64] {'page'}, use_global_device_ids=true, to_apply=%region_2.3 | all-reduce | flops 9216 | bytes 73728 | tf_op jit(solution)/shard_map/psum | solution.py:85
  267.1 39.7 %gather_fusion = bf16[2048,576]{1,0:T(8,128)(2,1)} fusion(bf16[4,8,128,576]{3,2,1,0:T(8,128)(2,1)} %copy.109, s32[2048]{0:T(1024)S(1)} %reshape.256), kind=kCustom, calls=%fused_computation | custom fusion | bytes 4743168 | tf_op jit(solution)/shard_map/vmap(vmap())/gather | solution.py:38
  307.2 2.8 select_reduce_fusion
  310.0 1.1 fusion.3
  311.2 8.8 reshape.249
  320.5 8.7 convolution_convert_fusion
  329.2 15.5 %reshape.250 = bf16[64,1,128,576]{3,2,0,1:T(8,128)(2,1)} reshape(bf16[64,73728]{1,0:T(8,128)(2,1)} %convolution_convert_fusion) | data formatting | bytes 18874368 | tf_op jit(solution)/shard_map/reshape | solution.py:188
  344.7 13.9 %copy.123 = bf16[64,1,128,576]{2,3,1,0:T(8,128)(2,1)} copy(bf16[64,1,128,576]{3,2,0,1:T(8,128)(2,1)} %reshape.250) | data formatting | bytes 18874368 | tf_op jit(solution)/shard_map/reshape | solution.py:188
  358.6 10.9 %all-to-all-start = ((bf16[64,1,128,576]{2,3,1,0:T(8,128)(2,1)}), bf16[64,1,128,576]{2,3,1,0:T(8,128)(2,1)}, u32[]{:S(2)}, u32[]{:S(2)}) async-start(bf16[64,1,128,576]{2,3,1,0:T(8,128)(2,1)} %copy.123), calls=%async_computation | async-start | bytes 18874368 | tf_op jit(solution)/shard_map/all_to_all | solution.py:187
  371.6 259.4 %all-gather.4 = f32[64,4,12]{2,1,0:T(4,128)S(1)} all-gather(f32[1,4,12]{2,1,0:T(4,128)S(1)} %bitcast.156), channel_id=3, replica_groups=mesh['head'=4,'page'=64] {'page'}, dimensions={0}, use_global_device_ids=true | all-gather | bytes 12480 | tf_op jit(solution)/shard_map/all_gather | solution.py:14
  631.0 47.8 %all-gather.3 = f32[64,4,12]{2,1,0:T(4,128)S(1)} all-gather(f32[1,4,12]{2,1,0:T(4,128)S(1)} %bitcast.154), channel_id=2, replica_groups=mesh['head'=4,'page'=64] {'page'}, dimensions={0}, use_global_device_ids=true | all-gather | bytes 12480 | tf_op jit(solution)/shard_map/all_gather | solution.py:14
  680.5 66.4 %while.19 = (s32[]{:T(128)}, f32[4,12]{1,0:T(4,128)S(1)}, f32[4,12]{1,0:T(4,128)S(1)}, f32[4,12,512]{2,1,0:T(8,128)S(1)}, f32[64,4,12]{2,1,0:T(4,128)S(1)}, /*in...) while((s32[]{:T(128)}, f32[4,12]{1,0:T(4,128)S(1)}, ...), condition=%wide.region_6.7_spmd, body=%wide.region_5.6_spmd.sunk | while | flops 74021 | bytes 296983 | solution.py:19
  680.6 1.0 fusion.118
  681.6 1.0 fusion.118
  682.7 1.0 fusion.118
  683.7 1.0 fusion.118
  684.8 1.0 fusion.118
  685.8 1.0 fusion.118
  686.9 1.0 fusion.118
  689.0 1.0 fusion.118
  691.1 1.0 fusion.118
  693.2 1.0 fusion.118
  695.3 1.0 fusion.118
  697.4 1.0 fusion.118
  698.5 1.0 fusion.118
  699.5 1.0 fusion.118
  700.6 1.0 fusion.118
  701.6 1.0 fusion.118
  702.7 1.0 fusion.118
  703.8 1.0 fusion.118
  704.8 1.0 fusion.118
  705.9 1.0 fusion.118
  706.9 1.0 fusion.118
  709.0 1.0 fusion.118
  711.1 1.0 fusion.118
  713.2 1.0 fusion.118
  715.4 1.0 fusion.118
  717.5 1.0 fusion.118
  718.5 1.0 fusion.118
  719.6 1.0 fusion.118
  720.6 1.0 fusion.118
  721.7 1.0 fusion.118
  722.7 1.0 fusion.118
  723.8 1.0 fusion.118
  724.8 1.0 fusion.118
  725.9 1.0 fusion.118
  726.9 1.0 fusion.118
  729.1 1.0 fusion.118
  731.2 1.0 fusion.118
  733.3 1.0 fusion.118
  735.4 1.0 fusion.118
  737.5 1.0 fusion.118
  746.9 1.3 fusion.23
  748.8 75.9 %psum.22 = bf16[12,2048]{1,0:T(8,128)(2,1)S(1)} all-reduce(f32[12,2048]{1,0:T(8,128)S(1)} %dynamic_update_slice.3), channel_id=1, replica_groups=mesh['head'=4,'page'=64] {'head','page'}, use_global_device_ids=true, to_apply=%region_7.8 | all-reduce | flops 24576 | bytes 147456 | tf_op jit(solution)/shard_map/psum | solution.py:124
  825.1 1.7 gather_fusion.1
  827.9 2.5 convolution_multiply_fusion
  830.4 73.9 %psum.23 = bf16[12,2048]{1,0:T(8,128)(2,1)} all-reduce(f32[12,2048]{1,0:T(8,128)S(1)} %convolution_multiply_fusion), channel_id=1, replica_groups=mesh['head'=4,'page'=64] {'head','page'}, use_global_device_ids=true, to_apply=%region_11.12 | all-reduce | flops 24576 | bytes 147456 | tf_op jit(solution)/shard_map/psum | solution.py:146
  904.3 14.1 %copy.124 = bf16[64,1,128,576]{3,2,0,1:T(8,128)(2,1)} copy(bf16[64,1,128,576]{2,3,1,0:T(8,128)(2,1)} %all-to-all-done) | data formatting | bytes 18874368 | tf_op jit(solution)/shard_map/all_to_all | solution.py:187
  918.4 15.3 %reshape.251 = bf16[64,73728]{1,0:T(8,128)(2,1)} reshape(bf16[64,1,128,576]{3,2,0,1:T(8,128)(2,1)} %copy.124) | data formatting | bytes 18874368 | tf_op jit(solution)/shard_map/reshape | solution.py:196
  933.6 8.0 convolution_convert_fusion.1
  941.7 8.8 reshape.252
  950.5 37.5 %gather_fusion.2 = bf16[2048,576]{1,0:T(8,128)(2,1)} fusion(bf16[32,128,576]{2,1,0:T(8,128)(2,1)} %reshape.252, s32[2048]{0:T(1024)S(1)} %reshape.268), kind=kCustom, calls=%fused_computation.2 | custom fusion | bytes 4734976 | tf_op jit(solution)/shard_map/vmap()/gather | solution.py:38
  (192 shorter events, 32.6 us)
Async XLA Ops:
  7.2 820.7 %copy-start = (bf16[1,352,2048]{2,1,0:T(8,128)(2,1)S(1)}, bf16[1,352,2048]{2,1,0:T(8,128)(2,1)}, u32[]{:S(2)}) copy-start(bf16[1,352,2048]{2,1,0:T(8,128)(2,1)} %param.35) | copy-start | bytes 4325380
  7.2 672.4 %all-gather.7.cloned.1.call-start = ((), (), s32[]{:S(2)}) async-start(), calls=%async_computation.1 | async-start | bytes 8519680 | tf_op jit(solution)/shard_map/all_gather | solution.py:14
  8.5 7.8 copy-start.8
  8.5 7.8 copy-start.11
  8.5 257.7 %copy-start.15 = (s32[12]{0:T(128)S(1)}, s32[12]{0:T(128)}, u32[]{:S(2)}) copy-start(s32[12]{0:T(128)} %param.26) | copy-start | bytes 148
  8.5 257.9 %copy-start.13 = (s32[4,8]{1,0:T(4,128)S(1)}, s32[4,8]{1,0:T(4,128)}, u32[]{:S(2)}) copy-start(s32[4,8]{1,0:T(4,128)} %param.25) | copy-start | bytes 388
  8.5 258.3 %copy-start.6 = (bf16[4,512,64]{1,2,0:T(8,128)(2,1)S(1)}, bf16[4,512,64]{1,2,0:T(8,128)(2,1)}, u32[]{:S(2)}) copy-start(bf16[4,512,64]{1,2,0:T(8,128)(2,1)} %param.28) | copy-start | bytes 786436
  267.1 39.8 %copy-start.5 = (bf16[4,128,512]{2,1,0:T(8,128)(2,1)S(1)}, bf16[4,128,512]{2,1,0:T(8,128)(2,1)}, u32[]{:S(2)}) copy-start(bf16[4,128,512]{2,1,0:T(8,128)(2,1)} %param.21) | copy-start | bytes 1572868
  306.8 3.2 copy-start.1
  311.2 8.8 copy-start.7
  358.6 10.9 %copy-start.12 = (bf16[2048]{0:T(1024)(128)(2,1)S(1)}, bf16[2048]{0:T(1024)(128)(2,1)}, u32[]{:S(2)}) copy-start(bf16[2048]{0:T(1024)(128)(2,1)} %param.30) | copy-start | bytes 12292
  358.6 10.9 %copy-start.9 = (s32[12,6]{0,1:T(8,128)S(1)}, s32[12,6]{0,1:T(8,128)}, u32[]{:S(2)}) copy-start(s32[12,6]{0,1:T(8,128)} %param.32) | copy-start | bytes 868
  358.6 12.2 %copy-start.4 = (s32[4,512,64]{1,2,0:T(8,128)S(1)}, s32[4,512,64]{1,2,0:T(8,128)}, u32[]{:S(2)}) copy-start(s32[4,512,64]{1,2,0:T(8,128)} %param.27) | copy-start | bytes 1572868
  358.6 545.7 %all-to-all-start = ((bf16[64,1,128,576]{2,3,1,0:T(8,128)(2,1)}), bf16[64,1,128,576]{2,3,1,0:T(8,128)(2,1)}, u32[]{:S(2)}, u32[]{:S(2)}) async-start(bf16[64,1,128,576]{2,3,1,0:T(8,128)(2,1)} %copy.123), calls=%async_computation | async-start | bytes 18874368 | tf_op jit(solution)/shard_map/all_to_all | solution.py:187
  370.8 377.4 %copy-start.10 = (bf16[512,32]{0,1:T(8,128)(2,1)S(1)}, bf16[512,32]{0,1:T(8,128)(2,1)}, u32[]{:S(2)}) copy-start(bf16[512,32]{0,1:T(8,128)(2,1)} %param.23) | copy-start | bytes 98308
  371.4 453.5 %copy-start.14 = (bf16[2048,64]{0,1:T(8,128)(2,1)S(1)}, bf16[2048,64]{0,1:T(8,128)(2,1)}, u32[]{:S(2)}) copy-start(bf16[2048,64]{0,1:T(8,128)(2,1)} %param.31) | copy-start | bytes 786436
  824.7 3.2 copy-start.3
  825.1 2.3 copy-start.2
Sparse Core Ops, SparseCore 0:
  311.3 121.7 all-gather.6
where the time goes:
time: 999 us; the launch traced here: 995 us
  blocking collectives  707 us (71%)
  local copies, waits for them, and re-layouts  168 us (17%)
  other arithmetic  66.3 us (7%)
  matrix products  26.8 us (3%)
  between operations  14.4 us (1%)
  starting transfers between devices  10.9 us (1%)
    all_gather x2, blocking collectives, joined_2(): gathered = jax.tree.map(lambda a: lax.all_gather(a, axis), part)  307 us
    psum x1, blocking collectives, shards(): lax.psum(partial_value, 'page').reshape(requests, heads_here, head_size)  250 us
    gather x4, local copies, waits for them, and re-layouts, pick_rows(): return one_page[row_ids]  77.4 us
    psum x1, blocking collectives, shards(): attn_out = lax.psum(padded, ('head', 'page')).astype(jnp.bfloat16)  75.9 us
    psum x1, blocking collectives, shards(): moe_out = lax.psum(expert_terms, ('head', 'page')).astype(jnp.bfloat16)  73.9 us
    add x63, other arithmetic, merge_parts(): left_part[2] * left_factor[..., None]  62.9 us
    reshape x2, local copies, waits for them, and re-layouts, shards(): outgoing.reshape(groups, sending_limit, page_rows, latent_dim)  29.4 us
  transfers between devices with their start and end apart: 2, of which 0 were waited for; matrix products, arithmetic and copies ran while one was open for 12% of the time, Pallas kernels for 0%

commit v1 on v0

--- a/solution.py
+++ b/solution.py
@@ -8,6 +8,12 @@
 THETA = 50000.0
 ROUTE_SCALE = 2.446
 NORM_EPS = 1e-06
+
+
+def add_all(block, axis):
+    pieces = lax.all_gather(block, axis, axis=0, tiled=False)
+    total = pieces.sum(axis=0)
+    return total
 
 
 def joined_2(part, axis, combine):
@@ -82,7 +88,7 @@
     sending_limit = (blocks + groups - 1) // groups
     first_page = page_index * pages_here
     partial_value = jnp.dot(hidden, q_weight, preferred_element_type=jnp.float32)
-    queries = lax.psum(partial_value, "page").reshape(requests, heads_here, head_size)
+    queries = add_all(partial_value, "page").reshape(requests, heads_here, head_size)
     q_nope = queries[..., :QK_NOPE].astype(jnp.bfloat16)
     positions = seq_pages * page_rows - 1
     q_rope = rotate_query(queries[..., QK_NOPE:], positions).astype(jnp.bfloat16)

time: 999 us -> 785 us (0.79)
  blocking collectives: 707 us -> 458 us
  waiting for transfers between devices: 0.02 us -> 35.5 us
    psum x1 -> x0, blocking collectives: 250 us -> none  [shards(): lax.psum(partial_value, 'page').reshape(requests, heads_here, head_size)]
    all_gather x0 -> x1, waiting for transfers between devices: none -> 35.4 us  [add_all(): pieces = lax.all_gather(block, axis, axis=0, tiled=False)]
  transfers between devices with their start and end apart: 2 -> 3, of which waited for: 0 -> 1; matrix products, arithmetic and copies ran while one was open for 12% -> 22% of each run, Pallas kernels for 0% -> 0%
where the time goes in v1:
time: 785 us; the launch traced here: 781 us
  blocking collectives  458 us (58%)
  local copies, waits for them, and re-layouts  168 us (21%)
  other arithmetic  68.2 us (9%)
  waiting for transfers between devices  35.5 us (5%)
  matrix products  28.3 us (4%)
  between operations  14.4 us (2%)
    all_gather x2, blocking collectives, joined_2(): gathered = jax.tree.map(lambda a: lax.all_gather(a, axis), part)  308 us
    gather x4, local copies, waits for them, and re-layouts, pick_rows(): return one_page[row_ids]  77.4 us
    psum x1, blocking collectives, shards(): attn_out = lax.psum(padded, ('head', 'page')).astype(jnp.bfloat16)  76.1 us
    psum x1, blocking collectives, shards(): moe_out = lax.psum(expert_terms, ('head', 'page')).astype(jnp.bfloat16)  74 us
    add x63, other arithmetic, merge_parts(): left_part[2] * left_factor[..., None]  62.9 us
    all_gather x1, waiting for transfers between devices, add_all(): pieces = lax.all_gather(block, axis, axis=0, tiled=False)  35.4 us
    reshape x2, local copies, waits for them, and re-layouts, shards(): outgoing.reshape(groups, sending_limit, page_rows, latent_dim)  29.4 us
  transfers between devices with their start and end apart: 3, of which 1 were waited for; matrix products, arithmetic and copies ran while one was open for 22% of the time, Pallas kernels for 0%

profile of v1, /device:TPU:1, one launch (start us, length us, event | category | flops | bytes accessed | tf_op | source)
XLA Modules:
  0.0 781.2 jit_solution(14526703988807643904)
XLA Ops:
  7.2 1.7 convolution_bitcast_fusion
  9.0 1.0 constant_dynamic-slice_fusion.2
  10.2 7.7 copy.117
  18.7 39.7 %gather_fusion = bf16[2048,576]{1,0:T(8,128)(2,1)} fusion(bf16[4,8,128,576]{3,2,1,0:T(8,128)(2,1)} %copy.117, s32[2048]{0:T(1024)S(1)} %reshape.256), kind=kCustom, calls=%fused_computation | custom fusion | bytes 4743168 | tf_op jit(solution)/shard_map/vmap(vmap())/gather | solution.py:44
  58.6 35.4 %all-gather.12.cloned.1.call-done = f32[64,12,768]{2,1,0:T(8,128)} async-done(((f32[1,12,768]{2,1,0:T(8,128)}), f32[64,12,768]{2,1,0:T(8,128)}) %all-gather.12.cloned.1.call-update) | async-done | bytes 2359312 | tf_op jit(solution)/shard_map/all_gather | solution.py:14
  94.0 2.1 reduce_sum.68
  96.5 2.8 select_reduce_fusion
  99.3 1.1 fusion.3
  100.4 8.8 %reshape.249 = bf16[32,73728]{1,0:T(8,128)(2,1)} reshape(bf16[4,8,128,576]{3,2,1,0:T(8,128)(2,1)} %copy.117) | data formatting | bytes 9437184 | tf_op jit(solution)/shard_map/reshape | solution.py:189
  109.7 8.8 %convolution_convert_fusion = bf16[64,73728]{1,0:T(8,128)(2,1)} fusion(bf16[32,73728]{1,0:T(8,128)(2,1)} %reshape.249, s32[32]{0:T(128)S(1)} %add_add_fusion.1), kind=kOutput, calls=%fused_computation.11 | convolution fusion | flops 306710528 | bytes 14155904 | tf_op jit(solution)/shard_map/bc,bx->cx/dot_general | solution.py:190
  118.4 15.5 %reshape.250 = bf16[64,1,128,576]{3,2,0,1:T(8,128)(2,1)} reshape(bf16[64,73728]{1,0:T(8,128)(2,1)} %convolution_convert_fusion) | data formatting | bytes 18874368 | tf_op jit(solution)/shard_map/reshape | solution.py:194
  133.9 13.9 %copy.131 = bf16[64,1,128,576]{2,3,1,0:T(8,128)(2,1)} copy(bf16[64,1,128,576]{3,2,0,1:T(8,128)(2,1)} %reshape.250) | data formatting | bytes 18874368 | tf_op jit(solution)/shard_map/reshape | solution.py:194
  147.9 6.6 all-to-all-start
  157.4 259.6 %all-gather.6 = f32[64,4,12]{2,1,0:T(4,128)S(1)} all-gather(f32[1,4,12]{2,1,0:T(4,128)S(1)} %bitcast.158), channel_id=4, replica_groups=mesh['head'=4,'page'=64] {'page'}, dimensions={0}, use_global_device_ids=true | all-gather | bytes 12480 | tf_op jit(solution)/shard_map/all_gather | solution.py:20
  417.0 48.7 %all-gather.5 = f32[64,4,12]{2,1,0:T(4,128)S(1)} all-gather(f32[1,4,12]{2,1,0:T(4,128)S(1)} %bitcast.156), channel_id=3, replica_groups=mesh['head'=4,'page'=64] {'page'}, dimensions={0}, use_global_device_ids=true | all-gather | bytes 12480 | tf_op jit(solution)/shard_map/all_gather | solution.py:20
  466.6 66.3 %while.19 = (s32[]{:T(128)}, f32[4,12]{1,0:T(4,128)S(1)}, f32[4,12]{1,0:T(4,128)S(1)}, f32[4,12,512]{2,1,0:T(8,128)S(1)}, f32[64,4,12]{2,1,0:T(4,128)S(1)}, /*in...) while((s32[]{:T(128)}, f32[4,12]{1,0:T(4,128)S(1)}, ...), condition=%wide.region_6.7_spmd, body=%wide.region_5.6_spmd.sunk | while | flops 74021 | bytes 296983 | solution.py:25
  466.7 1.0 fusion.123
  467.7 1.0 fusion.123
  468.8 1.0 fusion.123
  470.9 1.0 fusion.123
  471.9 1.0 fusion.123
  474.0 1.0 fusion.123
  475.1 1.0 fusion.123
  476.1 1.0 fusion.123
  478.3 1.0 fusion.123
  479.3 1.0 fusion.123
  480.4 1.0 fusion.123
  482.5 1.0 fusion.123
  483.5 1.0 fusion.123
  484.6 1.0 fusion.123
  486.7 1.0 fusion.123
  487.7 1.0 fusion.123
  488.8 1.0 fusion.123
  490.9 1.0 fusion.123
  491.9 1.0 fusion.123
  494.0 1.0 fusion.123
  495.1 1.0 fusion.123
  496.1 1.0 fusion.123
  498.2 1.0 fusion.123
  499.3 1.0 fusion.123
  500.3 1.0 fusion.123
  502.5 1.0 fusion.123
  503.5 1.0 fusion.123
  504.6 1.0 fusion.123
  506.7 1.0 fusion.123
  507.7 1.0 fusion.123
  508.8 1.0 fusion.123
  510.9 1.0 fusion.123
  511.9 1.0 fusion.123
  514.0 1.0 fusion.123
  515.1 1.0 fusion.123
  516.1 1.0 fusion.123
  518.2 1.0 fusion.123
  519.3 1.0 fusion.123
  532.9 1.3 fusion.23
  534.7 76.1 %psum.14 = bf16[12,2048]{1,0:T(8,128)(2,1)S(1)} all-reduce(f32[12,2048]{1,0:T(8,128)S(1)} %dynamic_update_slice.3), channel_id=1, replica_groups=mesh['head'=4,'page'=64] {'head','page'}, use_global_device_ids=true, to_apply=%region_7.8 | all-reduce | flops 24576 | bytes 147456 | tf_op jit(solution)/shard_map/psum | solution.py:130
  611.3 1.7 gather_fusion.1
  614.1 2.5 convolution_multiply_fusion
  616.6 74.0 %psum.15 = bf16[12,2048]{1,0:T(8,128)(2,1)} all-reduce(f32[12,2048]{1,0:T(8,128)S(1)} %convolution_multiply_fusion), channel_id=1, replica_groups=mesh['head'=4,'page'=64] {'head','page'}, use_global_device_ids=true, to_apply=%region_11.12 | all-reduce | flops 24576 | bytes 147456 | tf_op jit(solution)/shard_map/psum | solution.py:152
  690.6 14.1 %copy.132 = bf16[64,1,128,576]{3,2,0,1:T(8,128)(2,1)} copy(bf16[64,1,128,576]{2,3,1,0:T(8,128)(2,1)} %all-to-all-done) | data formatting | bytes 18874368 | tf_op jit(solution)/shard_map/all_to_all | solution.py:193
  704.7 15.3 %reshape.251 = bf16[64,73728]{1,0:T(8,128)(2,1)} reshape(bf16[64,1,128,576]{3,2,0,1:T(8,128)(2,1)} %copy.132) | data formatting | bytes 18874368 | tf_op jit(solution)/shard_map/reshape | solution.py:202
  720.0 8.0 %convolution_convert_fusion.1 = bf16[32,73728]{1,0:T(8,128)(2,1)} fusion(bf16[64,73728]{1,0:T(8,128)(2,1)} %reshape.251, s32[64,32]{1,0:T(8,128)S(1)} %add_add_fusion, s32[64,32]{1,0:T(8,128)S(1)} %copy.126, pred[64,32]{1,0:T(8,128)(4,1)S(1)} %copy.128), kind=kOutput, calls=%fused_computation.12 | convolution fusion | flops 313001984 | bytes 14174208 | tf_op jit(solution)/shard_map/dot_general | solution.py:200
  728.0 8.8 %reshape.252 = bf16[32,128,576]{2,1,0:T(8,128)(2,1)} reshape(bf16[32,73728]{1,0:T(8,128)(2,1)} %convolution_convert_fusion.1) | data formatting | bytes 9437184 | tf_op jit(solution)/shard_map/reshape | solution.py:206
  736.8 37.5 %gather_fusion.2 = bf16[2048,576]{1,0:T(8,128)(2,1)} fusion(bf16[32,128,576]{2,1,0:T(8,128)(2,1)} %reshape.252, s32[2048]{0:T(1024)S(1)} %reshape.268), kind=kCustom, calls=%fused_computation.2 | custom fusion | bytes 4734976 | tf_op jit(solution)/shard_map/vmap()/gather | solution.py:44
  (192 shorter events, 34.4 us)
Async XLA Ops:
  7.2 606.9 %copy-start = (bf16[1,352,2048]{2,1,0:T(8,128)(2,1)S(1)}, bf16[1,352,2048]{2,1,0:T(8,128)(2,1)}, u32[]{:S(2)}) copy-start(bf16[1,352,2048]{2,1,0:T(8,128)(2,1)} %param.35) | copy-start | bytes 4325380
  7.2 86.8 %all-gather.12.cloned.1.call-start = ((), (), s32[]{:S(2)}) async-start(), calls=%async_computation.2 | async-start | bytes 3194880 | tf_op jit(solution)/shard_map/all_gather | solution.py:14
  8.9 456.8 %all-gather.10.cloned.1.call-start = ((), (), s32[]{:S(2)}) async-start(), calls=%async_computation.1 | async-start | bytes 8519680 | tf_op jit(solution)/shard_map/all_gather | solution.py:20
  10.2 7.8 copy-start.13
  10.2 7.9 %copy-start.11 = (s32[4,8]{1,0:T(4,128)S(1)}, s32[4,8]{1,0:T(4,128)}, u32[]{:S(2)}) copy-start(s32[4,8]{1,0:T(4,128)} %param.25) | copy-start | bytes 388
  10.2 8.3 %copy-start.6 = (bf16[4,512,64]{1,2,0:T(8,128)(2,1)S(1)}, bf16[4,512,64]{1,2,0:T(8,128)(2,1)}, u32[]{:S(2)}) copy-start(bf16[4,512,64]{1,2,0:T(8,128)(2,1)} %param.28) | copy-start | bytes 786436
  58.4 37.8 %copy-start.5 = (bf16[4,128,512]{2,1,0:T(8,128)(2,1)S(1)}, bf16[4,128,512]{2,1,0:T(8,128)(2,1)}, u32[]{:S(2)}) copy-start(bf16[4,128,512]{2,1,0:T(8,128)(2,1)} %param.21) | copy-start | bytes 1572868
  96.2 3.1 copy-start.1
  100.4 8.8 %copy-start.7 = (s32[4,512]{1,0:T(4,128)S(1)}, s32[4,512]{1,0:T(4,128)}, u32[]{:S(2)}) copy-start(s32[4,512]{1,0:T(4,128)} %param.29) | copy-start | bytes 24580
  147.8 6.6 copy-start.10
  147.8 6.7 copy-start.8
  147.8 7.9 %copy-start.4 = (s32[4,512,64]{1,2,0:T(8,128)S(1)}, s32[4,512,64]{1,2,0:T(8,128)}, u32[]{:S(2)}) copy-start(s32[4,512,64]{1,2,0:T(8,128)} %param.27) | copy-start | bytes 1572868
  147.9 542.7 %all-to-all-start = ((bf16[64,1,128,576]{2,3,1,0:T(8,128)(2,1)}), bf16[64,1,128,576]{2,3,1,0:T(8,128)(2,1)}, u32[]{:S(2)}, u32[]{:S(2)}) async-start(bf16[64,1,128,576]{2,3,1,0:T(8,128)(2,1)} %copy.131), calls=%async_computation | async-start | bytes 18874368 | tf_op jit(solution)/shard_map/all_to_all | solution.py:193
  155.8 378.4 %copy-start.9 = (bf16[512,32]{0,1:T(8,128)(2,1)S(1)}, bf16[512,32]{0,1:T(8,128)(2,1)}, u32[]{:S(2)}) copy-start(bf16[512,32]{0,1:T(8,128)(2,1)} %param.23) | copy-start | bytes 98308
  156.4 454.7 %copy-start.12 = (bf16[2048,64]{0,1:T(8,128)(2,1)S(1)}, bf16[2048,64]{0,1:T(8,128)(2,1)}, u32[]{:S(2)}) copy-start(bf16[2048,64]{0,1:T(8,128)(2,1)} %param.31) | copy-start | bytes 786436
  610.9 3.2 copy-start.3
  611.3 2.3 copy-start.2
Sparse Core Ops, SparseCore 0:
  11.3 82.5 all-gather.11
  100.5 121.1 all-gather.9
